TPU v7x, 32 devices: a whole 2x2x4 slice. The times are simulated.
32 devices in a mesh: blk: 4 (over y, x), team: 4 (over z), dp: 2 (over core).
Axes of the slice: x: 2, y: 2, z: 4, core: 2. Of those that a mesh axis runs over, the one named last changes fastest.
Arguments:
- hidden: bfloat16 [1024, 28672], P(('blk', 'dp'), 'team'), may hold values from -6 to 6
- out_grad: bfloat16 [1024, 8192], P(('blk', 'dp'), 'team'), may hold values from -0.1875 to 0.1875
- act_rows: int32 [4, 64, 12], P('team'), may hold values from 0 to 55, as said below
- col_owner: int32 [64], replicated, may hold values from 0 to 3, as said below
Outputs:
- gradients: float32 [4, 4, 288, 128, 128], P('team', 'blk', 'dp')
- scores: float32 [4, 4, 288], P('team', 'blk', 'dp')
Inputs may be any that keep to these rules, and one draw needn't show every extreme that they name: For each t and c the 12 entries act_rows[t, c, :] are distinct. `col_owner`: some owner holds exactly 24 block columns and no owner holds more.
All inputs are finite; a program needn't handle non-finite values.
Results may differ from a plain program's by a relative error of at most 0.0003.
Values may be sent and summed in bfloat16 or wider, within the bound.
A program may use at most 192 MiB of HBM per device.

v0:
```python
import jax
import jax.numpy as jnp
from jax import lax
from jax.sharding import PartitionSpec as P

D = 8192
BS = 128
epsilon = 1e-06


def on_device(hidden, out_grad, act_rows, col_owner):
    owners_count = lax.axis_size("blk")
    owner_index = lax.axis_index("blk")
    column_blocks = D // BS
    capacity = min(3 * column_blocks // (2 * owners_count), 3 * column_blocks // 4)
    per_column = act_rows.shape[2]
    owners = jnp.arange(owners_count, dtype=jnp.int32)
    onehot = (col_owner[:, None] == owners[None, :]).astype(jnp.int32)
    column_rank = jnp.sum((jnp.cumsum(onehot, axis=0) - onehot) * onehot, axis=1)
    slot_ids = jnp.arange(capacity, dtype=jnp.int32)
    matches = (col_owner[None, None, :] == owners[:, None, None]) & (
        column_rank[None, None, :] == slot_ids[None, :, None]
    )
    owned_all = jnp.sum(
        matches.astype(jnp.int32) * jnp.arange(column_blocks, dtype=jnp.int32)[None, None, :],
        axis=2,
    )
    alive_all = jnp.any(matches, axis=2)
    owned_mine = lax.dynamic_index_in_dim(owned_all, owner_index, 0, keepdims=False)
    alive_mine = lax.dynamic_index_in_dim(alive_all, owner_index, 0, keepdims=False)
    block_rows = jnp.take(act_rows[0], owned_mine, axis=0).reshape(-1)
    grad_full = lax.all_gather(out_grad, "team", axis=1, tiled=True)
    grad_mask = alive_mine.astype(jnp.bfloat16)[None, :, None]
    hidden_piece = lax.all_gather(hidden, "blk", axis=0, tiled=True)
    grad_piece = lax.all_gather(grad_full, "blk", axis=0, tiled=True)
    count_rows = grad_piece.shape[0]
    picked_grad = (
        jnp.take(grad_piece.reshape(count_rows, column_blocks, BS), owned_mine, axis=1) * grad_mask
    )
    count_rows = hidden_piece.shape[0]
    hidden_blocks = hidden_piece.reshape(count_rows, -1, BS)
    picked_hidden = jnp.take(hidden_blocks, block_rows, axis=1).reshape(
        count_rows, capacity, per_column, BS
    )
    partial_value = jnp.einsum(
        "ncki,ncj->ckij", picked_hidden, picked_grad, preferred_element_type=jnp.float32
    )
    partial_value = partial_value.reshape(capacity * per_column, BS, BS)
    gradients = lax.psum_scatter(partial_value, "dp", scatter_dimension=0, tiled=True)
    scores = jnp.sqrt(jnp.mean(gradients * gradients, axis=(1, 2)) + epsilon)
    return (gradients[None, None], scores[None, None])


def solution(mesh):
    in_specs = (P(("blk", "dp"), "team"), P(("blk", "dp"), "team"), P("team", None, None), P())
    out_specs = (P("team", "blk", "dp", None, None), P("team", "blk", "dp"))
    return jax.shard_map(
        on_device, mesh=mesh, in_specs=in_specs, out_specs=out_specs, check_vma=False
    )
```

profile of v0, /device:TPU:0, one launch (start us, length us, event | category | flops | bytes accessed | tf_op | source)
XLA Modules:
  0.0 305.4 jit_solution(6852745690831261006)
XLA Ops:
  7.2 0.0 copy-start.1
  7.2 0.0 copy-start
  7.2 0.0 all-gather.6.cloned.1.call-start
  7.2 2.0 copy.20
  9.3 0.0 all-gather.6.cloned.1.call-update
  9.3 0.0 all-gather.4.cloned.1.call-start
  9.3 3.9 %copy.17 = bf16[128,7168]{0,1:T(8,128)(2,1)} copy(bf16[128,7168]{1,0:T(8,128)(2,1)} %param.4) | data formatting | bytes 3670016 | tf_op args[0]
  13.2 0.0 all-gather.4.cloned.1.call-update
  13.2 0.0 all-gather.8.cloned.1.call-start
  13.3 44.7 %all-gather.6.cloned.1.call-done = bf16[128,8192]{0,1:T(8,128)(2,1)} async-done(((bf16[128,2048]{0,1:T(8,128)(2,1)}), bf16[128,8192]{0,1:T(8,128)(2,1)}) %all-gather.6.cloned.1.call-update) | async-done | bytes 2097168 | tf_op jit(solution)/shard_map/all_gather | solution.py:32
  58.0 0.0 all-gather.8.cloned.1.call-update
  58.0 0.0 reduce-scatter.2.cloned.1.call-start
  58.1 0.0 copy-done.1
  58.1 0.1 fusion.11
  58.1 0.1 reduce_window_sum.11
  58.2 0.0 copy-done
  58.2 0.1 copy.16
  58.3 0.2 select_reduce_fusion
  58.5 0.1 fusion.10
  58.7 0.6 gather_fusion
  59.3 0.1 compare_and_fusion
  59.4 0.1 select_n.73
  59.5 0.2 and_reduce_fusion
  59.7 78.1 %all-gather.4.cloned.1.call-done = bf16[512,7168]{0,1:T(8,128)(2,1)} async-done(((bf16[128,7168]{0,1:T(8,128)(2,1)}), bf16[512,7168]{0,1:T(8,128)(2,1)}) %all-gather.4.cloned.1.call-update) | async-done | bytes 7340048 | tf_op jit(solution)/shard_map/all_gather | solution.py:34
  137.8 10.4 %copy.18 = bf16[512,56,128]{2,0,1:T(8,128)(2,1)} copy(bf16[512,56,128]{0,2,1:T(8,128)(2,1)} %bitcast.28) | data formatting | bytes 14680064 | tf_op jit(solution)/shard_map/reshape | solution.py:41
  148.3 18.8 %gather_fusion.1 = bf16[288,512,128]{2,1,0:T(8,128)(2,1)} fusion(bf16[512,56,128]{2,0,1:T(8,128)(2,1)} %copy.18, s32[1024]{0:T(1024)S(1)} %pad_clamp_fusion), kind=kCustom, calls=%fused_computation.1 | custom fusion | bytes 75498624 | tf_op jit(solution)/shard_map/jit(_take)/gather | solution.py:42
  167.1 48.8 %copy.19 = bf16[512,24,12,128]{0,3,2,1:T(8,128)(2,1)} copy(bf16[512,24,12,128]{3,0,2,1:T(8,128)(2,1)} %bitcast.24) | data formatting | bytes 75497472 | tf_op jit(solution)/shard_map/jit(_take)/gather | solution.py:42
  215.8 11.2 %all-gather.8.cloned.1.call-done = bf16[512,8192]{0,1:T(8,128)(2,1)} async-done(((bf16[128,8192]{0,1:T(8,128)(2,1)}), bf16[512,8192]{0,1:T(8,128)(2,1)}) %all-gather.8.cloned.1.call-update) | async-done | bytes 8388624 | tf_op jit(solution)/shard_map/all_gather | solution.py:35
  227.0 11.9 %copy.21 = bf16[512,64,128]{2,0,1:T(8,128)(2,1)} copy(bf16[512,64,128]{0,2,1:T(8,128)(2,1)} %bitcast.27) | data formatting | bytes 16777216 | tf_op jit(solution)/shard_map/reshape | solution.py:38
  238.9 4.5 %gather_fusion.2 = bf16[24,512,128]{2,1,0:T(8,128)(2,1)S(1)} fusion(bf16[512,64,128]{2,0,1:T(8,128)(2,1)} %copy.21, s32[1024]{0:T(1024)S(1)} %pad_clamp_fusion.1), kind=kCustom, calls=%fused_computation.2 | custom fusion | bytes 6291552 | tf_op jit(solution)/shard_map/jit(_take)/gather | solution.py:38
  243.5 23.4 %fusion = f32[24,12,128,128]{3,2,1,0:T(8,128)} fusion(bf16[512,24,12,128]{0,3,2,1:T(8,128)(2,1)} %copy.19, pred[24,12]{1,0:T(8,128)(4,1)S(1)} %get-tuple-element.2, bf16[24,512,128]{2,1,0:T(8,128)(2,1)S(1)} %gather_fusion.2, pred[24]{0:T(512)(128)(4,1)S(1)} %compare_and_fusion.1, bf16[24]{0:T(256)(128)(2,1)S(1)} %fusion.13), kind=kOutput, calls=%fused_computation.3 | convolution fusion | flops 4853858304 | bytes 59769192 | tf_op jit(solution)/shard_map/ncki,ncj->ckij/dot_general | solution.py:45
  266.8 0.0 reduce-scatter.2.cloned.1.call-update
  266.9 26.7 %reduce-scatter.2.cloned.1.call-done = f32[144,128,128]{2,1,0:T(8,128)} async-done(((f32[288,128,128]{2,1,0:T(8,128)}), f32[144,128,128]{2,1,0:T(8,128)}) %reduce-scatter.2.cloned.1.call-update) | async-done | bytes 9437200 | tf_op jit(solution)/shard_map/reduce_scatter | solution.py:49
  293.6 4.7 %multiply_reduce_fusion = f32[144]{0:T(256)S(1)} fusion(f32[144,128,128]{2,1,0:T(8,128)} %reduce-scatter.2.cloned.1.call-done), kind=kLoop, calls=%fused_computation.7 | loop fusion | flops 4718448 | bytes 9437760 | tf_op jit(solution)/shard_map/reduce_sum | solution.py:50
  298.3 0.6 add_sqrt_fusion
  (8 shorter events, 0.1 us)
Async XLA Ops:
  7.2 50.9 %copy-start.1 = (s32[64]{0:T(128)S(1)}, s32[64]{0:T(128)}, u32[]{:S(2)}) copy-start(s32[64]{0:T(128)} %param.7) | copy-start | bytes 772
  7.2 51.1 %copy-start = (s32[1,64,12]{1,0,2:T(1,128)S(1)}, s32[1,64,12]{1,0,2:T(1,128)}, u32[]{:S(2)}) copy-start(s32[1,64,12]{1,0,2:T(1,128)} %param.6) | copy-start | bytes 9220
  7.2 50.8 %all-gather.6.cloned.1.call-start = ((), (), s32[]{:S(2)}) async-start(), calls=%async_computation.2 | async-start | bytes 2621440 | tf_op jit(solution)/shard_map/all_gather | solution.py:32
  9.3 128.5 %all-gather.4.cloned.1.call-start = ((), (), s32[]{:S(2)}) async-start(), calls=%async_computation.1 | async-start | bytes 9175040 | tf_op jit(solution)/shard_map/all_gather | solution.py:34
  13.2 213.8 %all-gather.8.cloned.1.call-start = ((), (), s32[]{:S(2)}) async-start(), calls=%async_computation.3 | async-start | bytes 10485760 | tf_op jit(solution)/shard_map/all_gather | solution.py:35
  58.0 235.6 %reduce-scatter.2.cloned.1.call-start = ((), (), s32[]{:S(2)}) async-start(), calls=%async_computation.4 | async-start | bytes 28311552 | tf_op jit(solution)/shard_map/reduce_scatter | solution.py:49
Sparse Core Ops, SparseCore 0:
  9.6 48.3 all-gather.5
  60.4 77.4 all-gather.3
  139.7 87.3 all-gather.7
  267.0 26.5 reduce-scatter.1
where the time goes:
time: 307 us; the launch traced here: 305 us
  waiting for transfers between devices  161 us (52%)
  local copies, waits for them, and re-layouts  101 us (33%)
  matrix products  23.4 us (8%)
  between operations  13.9 us (5%)
  other arithmetic  6.12 us (2%)
    all_gather x1, waiting for transfers between devices, on_device(): hidden_piece = lax.all_gather(hidden, 'blk', axis=0, tiled=True)  78.1 us
    gather x2, local copies, waits for them, and re-layouts, on_device(): jnp.take(hidden_blocks, block_rows, axis=1)  67.6 us
    all_gather x1, waiting for transfers between devices, on_device(): grad_full = lax.all_gather(out_grad, 'team', axis=1, tiled=True)  44.7 us
    reduce_scatter x1, waiting for transfers between devices, on_device(): lax.psum_scatter(partial_value, 'dp', scatter_dimension=0, tiled=True)  26.7 us
    dot_general x1, matrix products, on_device(): jnp.einsum('ncki,ncj->ckij', picked_hidden, picked_grad, preferred_elemen...  23.4 us
    reshape x1, local copies, waits for them, and re-layouts, on_device(): grad_piece.reshape(count_rows, column_blocks, BS)  11.9 us
    all_gather x1, waiting for transfers between devices, on_device(): grad_piece = lax.all_gather(grad_full, 'blk', axis=0, tiled=True)  11.2 us
    reshape x1, local copies, waits for them, and re-layouts, on_device(): hidden_blocks = hidden_piece.reshape(count_rows, -1, BS)  10.4 us
  transfers between devices with their start and end apart: 4, of which 4 were waited for; matrix products, arithmetic and copies ran while one was open for 27% of the time, Pallas kernels for 0%

commit v1 on v0

--- a/solution.py
+++ b/solution.py
@@ -29,7 +29,12 @@
     owned_mine = lax.dynamic_index_in_dim(owned_all, owner_index, 0, keepdims=False)
     alive_mine = lax.dynamic_index_in_dim(alive_all, owner_index, 0, keepdims=False)
     block_rows = jnp.take(act_rows[0], owned_mine, axis=0).reshape(-1)
-    grad_full = lax.all_gather(out_grad, "team", axis=1, tiled=True)
+    ring = [out_grad]
+    for hop in range(3):
+        ring.append(lax.ppermute(ring[-1], "team", [(dev, (dev + 1) % 4) for dev in range(4)]))
+    grad_full = jnp.roll(
+        jnp.concatenate(ring[::-1], axis=1), (lax.axis_index("team") + 1) * ring[0].shape[1], axis=1
+    )
     grad_mask = alive_mine.astype(jnp.bfloat16)[None, :, None]
     hidden_piece = lax.all_gather(hidden, "blk", axis=0, tiled=True)
     grad_piece = lax.all_gather(grad_full, "blk", axis=0, tiled=True)

time: 307 us -> 262 us (0.85)
  waiting for transfers between devices: 161 us -> 112 us
    all_gather x1, waiting for transfers between devices: 78.1 us -> 31.4 us  [on_device(): hidden_piece = lax.all_gather(hidden, 'blk', axis=0, tiled=True)]
    all_gather x1 -> x0, waiting for transfers between devices: 44.7 us -> none  [on_device(): grad_full = lax.all_gather(out_grad, 'team', axis=1, tiled=True)]
    ppermute x0 -> x3, waiting for transfers between devices: none -> 42.9 us  [on_device(): lax.ppermute(ring[-1], 'team', [(dev, (dev + 1) % 4) for dev in range(4)])]
    ppermute x0 -> x3, starting transfers between devices: none -> 3.11 us  [on_device(): lax.ppermute(ring[-1], 'team', [(dev, (dev + 1) % 4) for dev in range(4)])]
  transfers between devices with their start and end apart: 4 -> 6, of which waited for: 4 -> 6; matrix products, arithmetic and copies ran while one was open for 27% -> 31% of each run, Pallas kernels for 0% -> 0%
where the time goes in v1:
time: 262 us; the launch traced here: 260 us
  waiting for transfers between devices  112 us (43%)
  local copies, waits for them, and re-layouts  101 us (39%)
  matrix products  23.4 us (9%)
  between operations  13.9 us (5%)
  other arithmetic  6.12 us (2%)
  starting transfers between devices  3.23 us (1%)
    gather x2, local copies, waits for them, and re-layouts, on_device(): jnp.take(hidden_blocks, block_rows, axis=1)  67.6 us
    ppermute x3, waiting for transfers between devices, on_device(): lax.ppermute(ring[-1], 'team', [(dev, (dev + 1) % 4) for dev in range(4)])  42.9 us
    all_gather x1, waiting for transfers between devices, on_device(): hidden_piece = lax.all_gather(hidden, 'blk', axis=0, tiled=True)  31.4 us
    reduce_scatter x1, waiting for transfers between devices, on_device(): lax.psum_scatter(partial_value, 'dp', scatter_dimension=0, tiled=True)  26.7 us
    dot_general x1, matrix products, on_device(): jnp.einsum('ncki,ncj->ckij', picked_hidden, picked_grad, preferred_elemen...  23.4 us
    reshape x1, local copies, waits for them, and re-layouts, on_device(): grad_piece.reshape(count_rows, column_blocks, BS)  11.9 us
    all_gather x1, waiting for transfers between devices, on_device(): grad_piece = lax.all_gather(grad_full, 'blk', axis=0, tiled=True)  11.2 us
    reshape x1, local copies, waits for them, and re-layouts, on_device(): hidden_blocks = hidden_piece.reshape(count_rows, -1, BS)  10.4 us
  transfers between devices with their start and end apart: 6, of which 6 were waited for; matrix products, arithmetic and copies ran while one was open for 31% of the time, Pallas kernels for 0%

profile of v1, /device:TPU:0, one launch (start us, length us, event | category | flops | bytes accessed | tf_op | source)
XLA Modules:
  0.0 260.3 jit_solution(9478248536741988886)
XLA Ops:
  7.2 0.0 copy-start
  7.2 0.0 all-gather.3.cloned.1.call-start
  7.2 3.9 %copy.19 = bf16[128,7168]{0,1:T(8,128)(2,1)} copy(bf16[128,7168]{1,0:T(8,128)(2,1)} %param.4) | data formatting | bytes 3670016 | tf_op args[0]
  11.1 0.0 all-gather.3.cloned.1.call-update
  11.2 0.0 all-gather.5.cloned.1.call-start
  11.2 0.0 copy-done
  11.2 0.3 copy.22
  11.5 3.1 %collective-permute-start = (bf16[128,2048]{0,1:T(8,128)(2,1)S(1)}, bf16[128,2048]{0,1:T(8,128)(2,1)S(1)}, u32[]{:S(2)}, u32[]{:S(2)}) collective-permute-start(bf16[128,2048]{0,1:T(8,128)(2,1)S(1)} %copy.22), channel_id=1, source_target_pairs={{0,2},{2,4},{4,6},{6,0},{1,3},{3,5},{5,7},{7,1},{8,10},{10,12},{12... | collective-permute-start | bytes 1572872 | tf_op jit(solution)/shard_map/ppermute | solution.py:34
  14.6 13.9 %collective-permute-done = bf16[128,2048]{0,1:T(8,128)(2,1)S(1)} collective-permute-done((bf16[128,2048]{0,1:T(8,128)(2,1)S(1)}, bf16[128,2048]{0,1:T(8,128)(2,1)S(1)}, u32[]{:S(2)}, u32[]{:S(2)}) %collective-permute-start) | collective-permute-done | bytes 524320 | tf_op jit(solution)/shard_map/ppermute | solution.py:34
  28.6 0.0 collective-permute-start.1
  28.6 14.9 %collective-permute-done.1 = bf16[128,2048]{0,1:T(8,128)(2,1)S(1)} collective-permute-done((bf16[128,2048]{0,1:T(8,128)(2,1)S(1)}, bf16[128,2048]{0,1:T(8,128)(2,1)S(1)}, u32[]{:S(2)}, u32[]{:S(2)}) %collective-permute-start.1) | collective-permute-done | bytes 524320 | tf_op jit(solution)/shard_map/ppermute | solution.py:34
  43.4 0.0 collective-permute-start.2
  43.4 14.0 %collective-permute-done.2 = bf16[128,2048]{0,1:T(8,128)(2,1)S(1)} collective-permute-done((bf16[128,2048]{0,1:T(8,128)(2,1)S(1)}, bf16[128,2048]{0,1:T(8,128)(2,1)S(1)}, u32[]{:S(2)}, u32[]{:S(2)}) %collective-permute-start.2) | collective-permute-done | bytes 524320 | tf_op jit(solution)/shard_map/ppermute | solution.py:34
  57.5 0.1 constant_dynamic-update-slice_fusion.6
  57.6 0.1 constant_dynamic-update-slice_fusion.5
  57.7 0.1 constant_dynamic-update-slice_fusion.4
  57.7 0.1 constant_dynamic-update-slice_fusion.3
  57.8 0.1 constant_dynamic-update-slice_fusion.2
  57.9 0.0 copy-start.1
  57.9 0.0 copy-start.2
  57.9 0.1 constant_dynamic-update-slice_fusion.1
  58.0 0.1 constant_dynamic-update-slice_fusion
  58.1 1.5 constant_dynamic-slice_fusion
  59.6 0.0 all-gather.5.cloned.1.call-update
  59.6 0.0 reduce-scatter.2.cloned.1.call-start
  59.6 0.0 copy-done.1
  59.6 0.1 copy.18
  59.7 0.0 copy-done.2
  59.7 0.1 fusion.11
  59.8 0.1 reduce_window_sum.11
  59.9 0.2 select_reduce_fusion
  60.1 0.1 fusion.10
  60.3 0.6 gather_fusion
  60.9 0.1 compare_and_fusion
  61.0 0.1 select_n.86
  61.1 0.2 and_reduce_fusion
  61.3 31.4 %all-gather.3.cloned.1.call-done = bf16[512,7168]{0,1:T(8,128)(2,1)} async-done(((bf16[128,7168]{0,1:T(8,128)(2,1)}), bf16[512,7168]{0,1:T(8,128)(2,1)}) %all-gather.3.cloned.1.call-update) | async-done | bytes 7340048 | tf_op jit(solution)/shard_map/all_gather | solution.py:39
  92.7 10.4 %copy.20 = bf16[512,56,128]{2,0,1:T(8,128)(2,1)} copy(bf16[512,56,128]{0,2,1:T(8,128)(2,1)} %bitcast.28) | data formatting | bytes 14680064 | tf_op jit(solution)/shard_map/reshape | solution.py:46
  103.1 18.8 %gather_fusion.1 = bf16[288,512,128]{2,1,0:T(8,128)(2,1)} fusion(bf16[512,56,128]{2,0,1:T(8,128)(2,1)} %copy.20, s32[1024]{0:T(1024)S(1)} %pad_clamp_fusion), kind=kCustom, calls=%fused_computation.1 | custom fusion | bytes 75498624 | tf_op jit(solution)/shard_map/jit(_take)/gather | solution.py:47
  121.9 48.8 %copy.21 = bf16[512,24,12,128]{0,3,2,1:T(8,128)(2,1)} copy(bf16[512,24,12,128]{3,0,2,1:T(8,128)(2,1)} %bitcast.24) | data formatting | bytes 75497472 | tf_op jit(solution)/shard_map/jit(_take)/gather | solution.py:47
  170.6 11.2 %all-gather.5.cloned.1.call-done = bf16[512,8192]{0,1:T(8,128)(2,1)} async-done(((bf16[128,8192]{0,1:T(8,128)(2,1)}), bf16[512,8192]{0,1:T(8,128)(2,1)}) %all-gather.5.cloned.1.call-update) | async-done | bytes 8388624 | tf_op jit(solution)/shard_map/all_gather | solution.py:40
  181.9 11.9 %copy.25 = bf16[512,64,128]{2,0,1:T(8,128)(2,1)} copy(bf16[512,64,128]{0,2,1:T(8,128)(2,1)} %bitcast.27) | data formatting | bytes 16777216 | tf_op jit(solution)/shard_map/reshape | solution.py:43
  193.8 4.5 %gather_fusion.2 = bf16[24,512,128]{2,1,0:T(8,128)(2,1)S(1)} fusion(bf16[512,64,128]{2,0,1:T(8,128)(2,1)} %copy.25, s32[1024]{0:T(1024)S(1)} %pad_clamp_fusion.1), kind=kCustom, calls=%fused_computation.2 | custom fusion | bytes 6291552 | tf_op jit(solution)/shard_map/jit(_take)/gather | solution.py:43
  198.3 23.4 %fusion = f32[24,12,128,128]{3,2,1,0:T(8,128)} fusion(bf16[512,24,12,128]{0,3,2,1:T(8,128)(2,1)} %copy.21, pred[24,12]{1,0:T(8,128)(4,1)S(1)} %get-tuple-element.2, bf16[24,512,128]{2,1,0:T(8,128)(2,1)S(1)} %gather_fusion.2, pred[24]{0:T(512)(128)(4,1)S(1)} %compare_and_fusion.1, bf16[24]{0:T(256)(128)(2,1)S(1)} %fusion.13), kind=kOutput, calls=%fused_computation.3 | convolution fusion | flops 4853858304 | bytes 59769192 | tf_op jit(solution)/shard_map/ncki,ncj->ckij/dot_general | solution.py:50
  221.7 0.0 reduce-scatter.2.cloned.1.call-update
  221.7 26.7 %reduce-scatter.2.cloned.1.call-done = f32[144,128,128]{2,1,0:T(8,128)} async-done(((f32[288,128,128]{2,1,0:T(8,128)}), f32[144,128,128]{2,1,0:T(8,128)}) %reduce-scatter.2.cloned.1.call-update) | async-done | bytes 9437200 | tf_op jit(solution)/shard_map/reduce_scatter | solution.py:54
  248.4 4.7 %multiply_reduce_fusion = f32[144]{0:T(256)S(1)} fusion(f32[144,128,128]{2,1,0:T(8,128)} %reduce-scatter.2.cloned.1.call-done), kind=kLoop, calls=%fused_computation.7 | loop fusion | flops 4718448 | bytes 9437760 | tf_op jit(solution)/shard_map/reduce_sum | solution.py:55
  253.1 0.6 add_sqrt_fusion
  (9 shorter events, 0.1 us)
Async XLA Ops:
  7.2 4.1 %copy-start = (bf16[128,2048]{1,0:T(8,128)(2,1)S(1)}, bf16[128,2048]{1,0:T(8,128)(2,1)}, u32[]{:S(2)}) copy-start(bf16[128,2048]{1,0:T(8,128)(2,1)} %param.5) | copy-start | bytes 1572868
  7.2 85.5 %all-gather.3.cloned.1.call-start = ((), (), s32[]{:S(2)}) async-start(), calls=%async_computation.1 | async-start | bytes 9175040 | tf_op jit(solution)/shard_map/all_gather | solution.py:39
  11.2 170.7 %all-gather.5.cloned.1.call-start = ((), (), s32[]{:S(2)}) async-start(), calls=%async_computation.2 | async-start | bytes 10485760 | tf_op jit(solution)/shard_map/all_gather | solution.py:40
  11.5 17.1 %collective-permute-start = (bf16[128,2048]{0,1:T(8,128)(2,1)S(1)}, bf16[128,2048]{0,1:T(8,128)(2,1)S(1)}, u32[]{:S(2)}, u32[]{:S(2)}) collective-permute-start(bf16[128,2048]{0,1:T(8,128)(2,1)S(1)} %copy.22), channel_id=1, source_target_pairs={{0,2},{2,4},{4,6},{6,0},{1,3},{3,5},{5,7},{7,1},{8,10},{10,12},{12... | collective-permute-start | bytes 1572872 | tf_op jit(solution)/shard_map/ppermute | solution.py:34
  28.6 14.9 %collective-permute-start.1 = (bf16[128,2048]{0,1:T(8,128)(2,1)S(1)}, bf16[128,2048]{0,1:T(8,128)(2,1)S(1)}, u32[]{:S(2)}, u32[]{:S(2)}) collective-permute-start(bf16[128,2048]{0,1:T(8,128)(2,1)S(1)} %collective-permute-done), channel_id=1, source_target_pairs={{0,2},{2,4},{4,6},{6,0},{1,3},{3,5},{5,7},{7,1},{8,10},{10,12},{12... | collective-permute-start | bytes 1572872 | tf_op jit(solution)/shard_map/ppermute | solution.py:34
  43.4 14.0 %collective-permute-start.2 = (bf16[128,2048]{0,1:T(8,128)(2,1)S(1)}, bf16[128,2048]{0,1:T(8,128)(2,1)S(1)}, u32[]{:S(2)}, u32[]{:S(2)}) collective-permute-start(bf16[128,2048]{0,1:T(8,128)(2,1)S(1)} %collective-permute-done.1), channel_id=1, source_target_pairs={{0,2},{2,4},{4,6},{6,0},{1,3},{3,5},{5,7},{7,1},{8,10},{10,12},{12... | collective-permute-start | bytes 1572872 | tf_op jit(solution)/shard_map/ppermute | solution.py:34
  57.9 1.7 copy-start.1
  57.9 1.8 copy-start.2
  59.6 188.8 %reduce-scatter.2.cloned.1.call-start = ((), (), s32[]{:S(2)}) async-start(), calls=%async_computation.3 | async-start | bytes 28311552 | tf_op jit(solution)/shard_map/reduce_scatter | solution.py:54
Sparse Core Ops, SparseCore 0:
  11.3 81.3 all-gather.2
  94.5 87.3 all-gather.4
  221.8 26.5 reduce-scatter.1
